TPU v7x, 32 devices: a whole 2x2x4 slice. The times are simulated.
32 devices in a mesh: dp: 8 (over z, x), tensor: 4 (over y, core).
Axes of the slice: x: 2, y: 2, z: 4, core: 2. Of those that a mesh axis runs over, the one named last changes fastest.
Arguments:
- tokens: bfloat16 [16384, 768], P('dp'), may hold values from -6 to 6
- seq_lengths: int32 [8, 9], P('dp'), may hold values from 1 to 512, 2048 in all within a row
- query_weight: bfloat16 [768, 768], P(None, 'tensor'), may hold values from -0.21875 to 0.21875
- key_weight: bfloat16 [768, 768], P(None, 'tensor'), may hold values from -0.21875 to 0.21875
- value_weight: bfloat16 [768, 768], P(None, 'tensor'), may hold values from -0.21875 to 0.21875
- out_weight: bfloat16 [768, 768], P('tensor'), may hold values from -0.875 to 0.875
- ffn_in: bfloat16 [768, 3072], P(None, 'tensor'), may hold values from -0.21875 to 0.21875
- ffn_out: bfloat16 [3072, 768], P('tensor'), may hold values from -0.109375 to 0.109375
- gain_attn: float32 [768], replicated, may hold values from 0.5 to 1.5
- gain_ffn: float32 [768], replicated, may hold values from 0.5 to 1.5
- query_down: bfloat16 [768, 8], replicated, may hold values from -0.21875 to 0.21875
- value_down: bfloat16 [768, 8], replicated, may hold values from -0.21875 to 0.21875
- query_up: bfloat16 [8, 12, 64], P(None, 'tensor'), may hold values from -1.078125 to 1.078125
- value_up: bfloat16 [8, 12, 64], P(None, 'tensor'), may hold values from -1.078125 to 1.078125
- cotangent: bfloat16 [16384, 768], P('dp'), may hold values from -6 to 6
Outputs:
- activations: bfloat16 [16384, 768], P(('dp', 'tensor'))
- input_grad: float32 [16384, 768], P(('dp', 'tensor'))
- query_up_grad: float32 [8, 12, 64], P(None, 'tensor', 'dp')
- value_up_grad: float32 [8, 12, 64], P(None, 'tensor', 'dp')
Inputs may be any that keep to these rules, and one draw needn't show every extreme that they name: `seq_lengths`: row b holds the lengths of the 8 sequences packed from the start of the b-th block of 2048 slots, in order, then the number of padding slots at the block's end; every row sums to 2048 and reaches 512.
All inputs are finite; a program needn't handle non-finite values.
Results may differ from a plain program's by a relative error of at most 0.025.
Values may be sent and summed in bfloat16 or wider, within the bound.
A program may use at most 128 MiB of HBM per device.

v0:
```python
import jax
import jax.numpy as jnp
from jax import lax
from jax.sharding import PartitionSpec as P

H = 12
HD = 64
R = 8
SEQ = 512
EPSILON = 1e-05
NEGATIVE = -1e30


def normalize(vector, scale_gain):
    average = jnp.mean(vector, axis=-1, keepdims=True)
    centered = vector - average
    inverse = lax.rsqrt(jnp.mean(centered * centered, axis=-1, keepdims=True) + EPSILON)
    unit_rows = centered * inverse
    return (unit_rows * scale_gain, unit_rows, inverse)


def normalize_back(upstream, unit_rows, inverse, scale_gain):
    scaled = upstream * scale_gain
    return inverse * (
        scaled
        - jnp.mean(scaled, axis=-1, keepdims=True)
        - unit_rows * jnp.mean(scaled * unit_rows, axis=-1, keepdims=True)
    )


def segment_ids(seg_ends, positions, block_rows):
    counted = jnp.sum((positions[:, None] >= seg_ends[None, :]).astype(jnp.int32), axis=1)
    inside = (positions >= 0) & (positions < block_rows)
    segment = jnp.where(inside, counted, -2)
    is_valid = inside & (counted < seg_ends.shape[0] - 1)
    return (segment, is_valid)


def transpose_dot(left_side, right_side):
    return lax.dot_general(
        left_side, right_side, (((1,), (1,)), ((), ())), preferred_element_type=jnp.float32
    )


def block_scores(
    block_index,
    queries,
    keys_ext,
    values_ext,
    seg_query,
    seg_keys,
    valid_query,
    head_count,
    block_span,
):
    col_width = queries.shape[1]
    head_size = col_width // head_count
    row_start = block_index * block_span
    query_block = lax.dynamic_slice_in_dim(queries, row_start, block_span, 0).reshape(
        block_span, head_count, head_size
    )
    key_block = lax.dynamic_slice_in_dim(keys_ext, row_start, 3 * block_span, 0).reshape(
        3 * block_span, head_count, head_size
    )
    value_block = lax.dynamic_slice_in_dim(values_ext, row_start, 3 * block_span, 0).reshape(
        3 * block_span, head_count, head_size
    )
    seg_rows = lax.dynamic_slice_in_dim(seg_query, row_start, block_span, 0)
    seg_cols = lax.dynamic_slice_in_dim(seg_keys, row_start, 3 * block_span, 0)
    valid_rows = lax.dynamic_slice_in_dim(valid_query, row_start, block_span, 0)
    allowed = (seg_rows[:, None] == seg_cols[None, :]) & valid_rows[:, None]
    scores = jnp.einsum(
        "qhd,khd->hqk", query_block, key_block, preferred_element_type=jnp.float32
    ) * head_size ** (-0.5)
    masked = jnp.where(allowed[None], scores, NEGATIVE)
    return (query_block, key_block, value_block, allowed, masked, valid_rows)


def attend_forward(
    block_index,
    queries,
    keys_ext,
    values_ext,
    seg_query,
    seg_keys,
    valid_query,
    head_count,
    block_span,
):
    query_block, key_block, value_block, allowed, masked, valid_rows = block_scores(
        block_index,
        queries,
        keys_ext,
        values_ext,
        seg_query,
        seg_keys,
        valid_query,
        head_count,
        block_span,
    )
    row_max = jnp.max(masked, axis=-1, keepdims=True)
    weights = jnp.where(allowed[None], jnp.exp(masked - row_max), 0.0)
    row_total = (
        jnp.sum(weights, axis=-1, keepdims=True)
        + (1.0 - valid_rows.astype(jnp.float32))[None, :, None]
    )
    probability = (weights / row_total).astype(jnp.bfloat16)
    mixed_rows = jnp.einsum(
        "hqk,khd->qhd", probability, value_block, preferred_element_type=jnp.float32
    )
    return (
        mixed_rows.reshape(block_span, queries.shape[1]),
        (row_max + jnp.log(row_total))[:, :, 0],
    )


def attend_backward(
    block_index,
    queries,
    keys_ext,
    values_ext,
    seg_query,
    seg_keys,
    valid_query,
    head_count,
    block_span,
    log_total,
    grad_context,
):
    query_block, key_block, value_block, allowed, masked, valid_rows = block_scores(
        block_index,
        queries,
        keys_ext,
        values_ext,
        seg_query,
        seg_keys,
        valid_query,
        head_count,
        block_span,
    )
    col_width = queries.shape[1]
    head_size = col_width // head_count
    score_scale = head_size ** (-0.5)
    stored = log_total[block_index]
    probability = jnp.where(allowed[None], jnp.exp(masked - stored[:, :, None]), 0.0)
    grad_block = lax.dynamic_slice_in_dim(
        grad_context, block_index * block_span, block_span, 0
    ).reshape(block_span, head_count, head_size)
    grad_prob = jnp.einsum(
        "qhd,khd->hqk", grad_block, value_block, preferred_element_type=jnp.float32
    )
    row_delta = jnp.sum(probability * grad_prob, axis=-1, keepdims=True)
    grad_scores = (probability * (grad_prob - row_delta)).astype(jnp.bfloat16)
    grad_query = (
        jnp.einsum("hqk,khd->qhd", grad_scores, key_block, preferred_element_type=jnp.float32)
        * score_scale
    )
    grad_key = (
        jnp.einsum("hqk,qhd->khd", grad_scores, query_block, preferred_element_type=jnp.float32)
        * score_scale
    )
    grad_value = jnp.einsum(
        "hqk,qhd->khd",
        probability.astype(jnp.bfloat16),
        grad_block,
        preferred_element_type=jnp.float32,
    )
    return (
        grad_query.reshape(block_span, col_width),
        grad_key.reshape(3 * block_span, col_width),
        grad_value.reshape(3 * block_span, col_width),
    )


def on_device(
    tokens,
    seq_lengths,
    query_weight,
    key_weight,
    value_weight,
    out_weight,
    ffn_in,
    ffn_out,
    gain_attn,
    gain_ffn,
    query_down,
    value_down,
    query_up,
    value_up,
    cotangent,
):
    groups = lax.axis_size("tensor")
    member = lax.axis_index("tensor")
    block_span = SEQ
    block_rows = tokens.shape[0]
    own_rows = block_rows // groups
    seg_ends = jnp.cumsum(seq_lengths[0])
    w_query, w_key, w_value, w_inner, w_out, w_ffn_out, up_query, up_value = (
        query_weight,
        key_weight,
        value_weight,
        ffn_in,
        out_weight,
        ffn_out,
        query_up,
        value_up,
    )
    first_row = 0
    head_count = H // groups
    row_count = tokens.shape[0]
    col_width = w_query.shape[1]
    up_query_flat = up_query.reshape(R, col_width)
    up_value_flat = up_value.reshape(R, col_width)
    down_query_wide = query_down.astype(jnp.float32)
    down_value_wide = value_down.astype(jnp.float32)
    low_query = jnp.dot(tokens, query_down, preferred_element_type=jnp.float32).astype(jnp.bfloat16)
    low_value = jnp.dot(tokens, value_down, preferred_element_type=jnp.float32).astype(jnp.bfloat16)
    queries = (
        jnp.dot(tokens, w_query, preferred_element_type=jnp.float32)
        + 2.0 * jnp.dot(low_query, up_query_flat, preferred_element_type=jnp.float32)
    ).astype(jnp.bfloat16)
    key_rows = jnp.dot(tokens, w_key, preferred_element_type=jnp.float32).astype(jnp.bfloat16)
    values = (
        jnp.dot(tokens, w_value, preferred_element_type=jnp.float32)
        + 2.0 * jnp.dot(low_value, up_value_flat, preferred_element_type=jnp.float32)
    ).astype(jnp.bfloat16)
    key_value = jnp.stack([key_rows, values])
    key_value_ext = jnp.pad(key_value, ((0, 0), (block_span, block_span), (0, 0)))
    keys_ext = key_value_ext[0]
    values_ext = key_value_ext[1]
    positions = first_row - block_span + jnp.arange(row_count + 2 * block_span, dtype=jnp.int32)
    seg_keys, valid_keys = segment_ids(seg_ends, positions, block_rows)
    seg_query = seg_keys[block_span : block_span + row_count]
    valid_query = valid_keys[block_span : block_span + row_count]
    valid_rows = valid_query.astype(jnp.float32)[:, None]
    block_count = row_count // block_span

    def forward_block(block_index):
        return attend_forward(
            block_index,
            queries,
            keys_ext,
            values_ext,
            seg_query,
            seg_keys,
            valid_query,
            head_count,
            block_span,
        )

    context_blocks, log_total = lax.map(forward_block, jnp.arange(block_count))
    context = context_blocks.reshape(row_count, col_width).astype(jnp.bfloat16)
    attn_out = lax.psum(
        jnp.dot(context, w_out, preferred_element_type=jnp.float32).astype(jnp.bfloat16), "tensor"
    ).astype(jnp.float32)
    normed, unit_one, inverse_one = normalize(tokens.astype(jnp.float32) + attn_out, gain_attn)
    normed_low = normed.astype(jnp.bfloat16)
    pre_act = jnp.dot(normed_low, w_inner, preferred_element_type=jnp.float32)
    active = jax.nn.gelu(pre_act, approximate=False).astype(jnp.bfloat16)
    ffn_result = lax.psum(
        jnp.dot(active, w_ffn_out, preferred_element_type=jnp.float32).astype(jnp.bfloat16),
        "tensor",
    ).astype(jnp.float32)
    final_rows, unit_two, inverse_two = normalize(normed + ffn_result, gain_ffn)
    final_rows = final_rows * valid_rows
    grad_final = cotangent.astype(jnp.float32) * valid_rows
    grad_mid = normalize_back(grad_final, unit_two, inverse_two, gain_ffn)
    grad_active = transpose_dot(grad_mid.astype(jnp.bfloat16), w_ffn_out)
    recomputed = jnp.dot(
        lax.optimization_barrier(normed_low), w_inner, preferred_element_type=jnp.float32
    )
    gelu_pull = jax.vjp(lambda argument: jax.nn.gelu(argument, approximate=False), recomputed)[1]
    grad_pre = gelu_pull(grad_active)[0].astype(jnp.bfloat16)
    grad_normed = grad_mid + lax.psum(
        transpose_dot(grad_pre, w_inner).astype(jnp.bfloat16), "tensor"
    ).astype(jnp.float32)
    grad_mixed = normalize_back(grad_normed, unit_one, inverse_one, gain_attn)
    grad_context = transpose_dot(grad_mixed.astype(jnp.bfloat16), w_out).astype(jnp.bfloat16)

    def back_step(accumulated, block_index):
        key_total, value_total = accumulated
        grad_query, grad_key, grad_value = attend_backward(
            block_index,
            queries,
            keys_ext,
            values_ext,
            seg_query,
            seg_keys,
            valid_query,
            head_count,
            block_span,
            log_total,
            grad_context,
        )
        row_start = block_index * block_span
        key_total = lax.dynamic_update_slice_in_dim(
            key_total,
            lax.dynamic_slice_in_dim(key_total, row_start, 3 * block_span, 0) + grad_key,
            row_start,
            0,
        )
        value_total = lax.dynamic_update_slice_in_dim(
            value_total,
            lax.dynamic_slice_in_dim(value_total, row_start, 3 * block_span, 0) + grad_value,
            row_start,
            0,
        )
        return ((key_total, value_total), grad_query)

    empty_ext = jnp.zeros((row_count + 2 * block_span, col_width), jnp.float32)
    (key_total, value_total), query_grads = lax.scan(
        back_step, (empty_ext, empty_ext), jnp.arange(block_count)
    )
    key_middle = key_total[block_span : block_span + row_count]
    value_middle = value_total[block_span : block_span + row_count]
    grad_queries = query_grads.reshape(row_count, col_width).astype(jnp.bfloat16)
    grad_keys = key_middle.astype(jnp.bfloat16)
    grad_values = value_middle.astype(jnp.bfloat16)
    input_term = (
        transpose_dot(grad_queries, w_query)
        + transpose_dot(grad_keys, w_key)
        + transpose_dot(grad_values, w_value)
    )
    low_query_grad = 2.0 * transpose_dot(grad_queries, up_query_flat)
    low_value_grad = 2.0 * transpose_dot(grad_values, up_value_flat)
    input_term = input_term + jnp.dot(
        low_query_grad,
        down_query_wide.T,
        precision=lax.Precision.HIGHEST,
        preferred_element_type=jnp.float32,
    )
    input_term = input_term + jnp.dot(
        low_value_grad,
        down_value_wide.T,
        precision=lax.Precision.HIGHEST,
        preferred_element_type=jnp.float32,
    )
    grad_input = grad_mixed + lax.psum(input_term.astype(jnp.bfloat16), "tensor").astype(
        jnp.float32
    )
    adapter_query = (
        2.0
        * lax.dot_general(
            low_query, grad_queries, (((0,), (0,)), ((), ())), preferred_element_type=jnp.float32
        )
    ).reshape(R, head_count, HD)
    adapter_value = (
        2.0
        * lax.dot_general(
            low_value, grad_values, (((0,), (0,)), ((), ())), preferred_element_type=jnp.float32
        )
    ).reshape(R, head_count, HD)
    grad_up_query, grad_up_value = (
        lax.psum_scatter(adapter_query, "dp", scatter_dimension=2, tiled=True),
        lax.psum_scatter(adapter_value, "dp", scatter_dimension=2, tiled=True),
    )
    out_rows = lax.dynamic_slice_in_dim(final_rows, member * own_rows, own_rows, 0).astype(
        jnp.bfloat16
    )
    out_grads = lax.dynamic_slice_in_dim(grad_input, member * own_rows, own_rows, 0)
    return (out_rows, out_grads, grad_up_query, grad_up_value)


def solution(mesh):
    in_specs = (
        P("dp", None),
        P("dp", None),
        P(None, "tensor"),
        P(None, "tensor"),
        P(None, "tensor"),
        P("tensor", None),
        P(None, "tensor"),
        P("tensor", None),
        P(),
        P(),
        P(),
        P(),
        P(None, "tensor", None),
        P(None, "tensor", None),
        P("dp", None),
    )
    out_specs = (
        P(("dp", "tensor"), None),
        P(("dp", "tensor"), None),
        P(None, "tensor", "dp"),
        P(None, "tensor", "dp"),
    )
    return jax.shard_map(
        on_device, mesh=mesh, in_specs=in_specs, out_specs=out_specs, check_vma=False
    )
```

profile of v0, /device:TPU:0, one launch (start us, length us, event | category | flops | bytes accessed | tf_op | source)
XLA Modules:
  0.0 639.0 jit_solution(7620324804941043654)
XLA Ops:
  23.7 58.6 %while.26 = (s32[]{:T(128)}, bf16[4,512,192]{1,2,0:T(8,128)(2,1)}, f32[4,3,512]{2,1,0:T(4,128)}, s32[4]{0:T(128)S(1)}, bf16[3072,192]{0,1:T(8,128)(2,1)S(1)}, /*...) while((s32[]{:T(128)}, bf16[4,512,192]{1,2,0:T(8,128)(2,1)}, ...), condition=%wide.region_5.6_spmd, body=%wide.region_2.5_spmd.sunk | while | flops 638585344 | bytes 36271876 | solution.py:251
  88.1 71.0 %all-reduce.9.cloned.1.call-done = bf16[2048,768]{1,0:T(8,128)(2,1)} async-done(((bf16[2048,768]{1,0:T(8,128)(2,1)}), bf16[2048,768]{1,0:T(8,128)(2,1)}) %all-reduce.9.cloned.1.call-update) | async-done | bytes 3145744 | tf_op jit(solution)/shard_map/psum | solution.py:253
  168.0 19.9 %convolution_convert_fusion.1 = bf16[2048,768]{1,0:T(8,128)(2,1)} fusion(bf16[768,768]{1,0:T(8,128)(2,1)S(1)} %copy-done.48, bf16[2048,768]{1,0:T(8,128)(2,1)} %multiply_convert_fusion.1, bf16[768,768]{1,0:T(8,128)(2,1)S(1)} %copy-done), kind=kOutput, calls=%fused_computation.101 | convolution fusion | flops 4935647232 | bytes 8650752 | tf_op jit(solution)/shard_map/dot_general | solution.py:261
  188.4 7.1 %fusion.131 = f32[2048,768]{1,0:T(8,128)} fusion(bf16[2048,768]{1,0:T(8,128)(2,1)} %multiply_convert_fusion.1, bf16[768,768]{1,0:T(8,128)(2,1)S(1)} %copy-done), kind=kOutput, calls=%fused_computation.218 | convolution fusion | flops 2415919104 | bytes 10616832 | tf_op jit(solution)/shard_map/dot_general | solution.py:269
  195.5 61.1 %all-reduce.11.cloned.1.call-done = bf16[2048,768]{1,0:T(8,128)(2,1)} async-done(((bf16[2048,768]{1,0:T(8,128)(2,1)}), bf16[2048,768]{1,0:T(8,128)(2,1)}) %all-reduce.11.cloned.1.call-update) | async-done | bytes 3145744 | tf_op jit(solution)/shard_map/psum | solution.py:260
  256.6 5.9 fusion.58
  277.4 22.6 %convolution_convert_fusion = bf16[2048,768]{1,0:T(8,128)(2,1)} fusion(bf16[768,768]{1,0:T(8,128)(2,1)S(1)} %copy-done, f32[2048,768]{1,0:T(8,128)} %fusion.131, bf16[768,768]{1,0:T(8,128)(2,1)S(1)} %copy-done.48, f32[2048,768]{1,0:T(8,128)} %subtract_multiply_fusion.1), kind=kOutput, calls=%fused_computation.100 | convolution fusion | flops 4948230144 | bytes 18087936 | tf_op jit(solution)/shard_map/dot_general | solution.py:40
  300.0 68.6 %all-reduce.13.cloned.1.call-done = bf16[2048,768]{1,0:T(8,128)(2,1)} async-done(((bf16[2048,768]{1,0:T(8,128)(2,1)}), bf16[2048,768]{1,0:T(8,128)(2,1)}) %all-reduce.13.cloned.1.call-update) | async-done | bytes 3145744 | tf_op jit(solution)/shard_map/psum | solution.py:274
  368.7 8.4 %fusion.59 = (f32[2048]{0:T(1024)S(1)}, f32[2048]{0:T(1024)S(1)}) fusion(f32[768]{0:T(1024)S(1)} %copy-done.38, f32[2048,768]{1,0:T(8,128)} %subtract_multiply_fusion.1, bf16[2048,768]{1,0:T(8,128)(2,1)} %all-reduce.13.cloned.1.call-done, f32[2048]{0:T(1024)S(1)} %add_rsqrt_fusion.1, f32[2048]{0:T(1024)S(1)} %copy-done.33, ...), kind=kLoop, calls=%fused_computation.123 | loop fusion | flops 17297408 | bytes 15764480 | tf_op jit(solution)/shard_map/reduce_sum | solution.py:26
  377.1 5.2 subtract_multiply_fusion
  388.6 154.5 %while.27 = (s32[]{:T(128)}, f32[3072,192]{0,1:T(8,128)}, f32[3072,192]{0,1:T(8,128)S(1)}, bf16[4,512,192]{1,2,0:T(8,128)(2,1)}, s32[4]{0:T(128)}, /*index=5*/bf...) while((s32[]{:T(128)}, f32[3072,192]{0,1:T(8,128)}, ...), condition=%wide.region_19.20_spmd, body=%wide.region_17.19_spmd.sunk | while | flops 1536195072 | bytes 170713200 | solution.py:311
  400.6 6.7 %multiply_reduce_fusion.6 = (f32[3,512]{1,0:T(4,128)S(1)}, f32[3,512,1536]{2,1,0:T(8,128)}) fusion(f32[3,512,1536]{2,1,0:T(8,128)S(1)} %fusion.220, f32[3,512]{1,0:T(4,128)S(1)} %dynamic-slice_bitcast_fusion.2, bf16[512,3,64]{0,2,1:T(8,128)(2,1)S(1)} %bitcast.166, bf16[1536,3,64]{0,2,1:T(8,128)(2,1)S(1)} %bitcast.162, ...), kind=kOutput, calls=%fused_computation.21.clone.1 | convolution fusion | flops 316144128 | bytes 20459520 | tf_op jit(solution)/shard_map/while/body/eval_jaxpr/qhd,khd->hqk/dot_general | solution.py:72
  407.3 9.4 %multiply_convert_fusion.3 = bf16[3,512,1536]{2,1,0:T(8,128)(2,1)} fusion(f32[3,512,1536]{2,1,0:T(8,128)} %get-tuple-element.368, f32[3,512,1536]{2,1,0:T(8,128)} %copy-done.2, f32[3,512]{1,0:T(4,128)S(1)} %get-tuple-element.369), kind=kLoop, calls=%fused_computation.20.clone.1 | loop fusion | flops 7077888 | bytes 23599104 | tf_op jit(solution)/shard_map/while/body/eval_jaxpr/convert_element_type | solution.py:153
  416.7 4.9 fusion.221
  439.2 6.7 %multiply_reduce_fusion.6 = (f32[3,512]{1,0:T(4,128)S(1)}, f32[3,512,1536]{2,1,0:T(8,128)}) fusion(f32[3,512,1536]{2,1,0:T(8,128)S(1)} %fusion.220, f32[3,512]{1,0:T(4,128)S(1)} %dynamic-slice_bitcast_fusion.2, bf16[512,3,64]{0,2,1:T(8,128)(2,1)S(1)} %bitcast.166, bf16[1536,3,64]{0,2,1:T(8,128)(2,1)S(1)} %bitcast.162, ...), kind=kOutput, calls=%fused_computation.21.clone.1 | convolution fusion | flops 316144128 | bytes 20459520 | tf_op jit(solution)/shard_map/while/body/eval_jaxpr/qhd,khd->hqk/dot_general | solution.py:72
  445.9 9.4 %multiply_convert_fusion.3 = bf16[3,512,1536]{2,1,0:T(8,128)(2,1)} fusion(f32[3,512,1536]{2,1,0:T(8,128)} %get-tuple-element.368, f32[3,512,1536]{2,1,0:T(8,128)} %copy-done.2, f32[3,512]{1,0:T(4,128)S(1)} %get-tuple-element.369), kind=kLoop, calls=%fused_computation.20.clone.1 | loop fusion | flops 7077888 | bytes 23599104 | tf_op jit(solution)/shard_map/while/body/eval_jaxpr/convert_element_type | solution.py:153
  455.3 4.9 fusion.221
  477.8 6.7 %multiply_reduce_fusion.6 = (f32[3,512]{1,0:T(4,128)S(1)}, f32[3,512,1536]{2,1,0:T(8,128)}) fusion(f32[3,512,1536]{2,1,0:T(8,128)S(1)} %fusion.220, f32[3,512]{1,0:T(4,128)S(1)} %dynamic-slice_bitcast_fusion.2, bf16[512,3,64]{0,2,1:T(8,128)(2,1)S(1)} %bitcast.166, bf16[1536,3,64]{0,2,1:T(8,128)(2,1)S(1)} %bitcast.162, ...), kind=kOutput, calls=%fused_computation.21.clone.1 | convolution fusion | flops 316144128 | bytes 20459520 | tf_op jit(solution)/shard_map/while/body/eval_jaxpr/qhd,khd->hqk/dot_general | solution.py:72
  484.5 9.4 %multiply_convert_fusion.3 = bf16[3,512,1536]{2,1,0:T(8,128)(2,1)} fusion(f32[3,512,1536]{2,1,0:T(8,128)} %get-tuple-element.368, f32[3,512,1536]{2,1,0:T(8,128)} %copy-done.2, f32[3,512]{1,0:T(4,128)S(1)} %get-tuple-element.369), kind=kLoop, calls=%fused_computation.20.clone.1 | loop fusion | flops 7077888 | bytes 23599104 | tf_op jit(solution)/shard_map/while/body/eval_jaxpr/convert_element_type | solution.py:153
  516.3 6.7 %multiply_reduce_fusion.6 = (f32[3,512]{1,0:T(4,128)S(1)}, f32[3,512,1536]{2,1,0:T(8,128)}) fusion(f32[3,512,1536]{2,1,0:T(8,128)S(1)} %fusion.220, f32[3,512]{1,0:T(4,128)S(1)} %dynamic-slice_bitcast_fusion.2, bf16[512,3,64]{0,2,1:T(8,128)(2,1)S(1)} %bitcast.166, bf16[1536,3,64]{0,2,1:T(8,128)(2,1)S(1)} %bitcast.162, ...), kind=kOutput, calls=%fused_computation.21.clone.1 | convolution fusion | flops 316144128 | bytes 20459520 | tf_op jit(solution)/shard_map/while/body/eval_jaxpr/qhd,khd->hqk/dot_general | solution.py:72
  523.1 9.4 %multiply_convert_fusion.3 = bf16[3,512,1536]{2,1,0:T(8,128)(2,1)} fusion(f32[3,512,1536]{2,1,0:T(8,128)} %get-tuple-element.368, f32[3,512,1536]{2,1,0:T(8,128)} %copy-done.2, f32[3,512]{1,0:T(4,128)S(1)} %get-tuple-element.369), kind=kLoop, calls=%fused_computation.20.clone.1 | loop fusion | flops 7077888 | bytes 23599104 | tf_op jit(solution)/shard_map/while/body/eval_jaxpr/convert_element_type | solution.py:153
  552.6 7.9 %add_convert_fusion = bf16[2048,768]{1,0:T(8,128)(2,1)} fusion(f32[2048,768]{1,0:T(8,128)} %fusion.133, f32[2048,768]{1,0:T(8,128)S(1)} %fusion.125, f32[2048,768]{1,0:T(8,128)S(1)} %fusion.132, f32[2048,768]{1,0:T(8,128)S(1)} %fusion.62, f32[2048,8]{0,1:T(8,128)S(1)} %convolution_multiply_fusion.4, bf16[768,8]{0,1:T(8,128)(2,1)S(1)} %copy-done.40), kind=kOutput, calls=%fused_computation.50 | convolution fusion | flops 158859264 | bytes 28389376 | tf_op jit(solution)/shard_map/dot_general | solution.py:332
  570.4 37.0 %all-reduce.3 = (f32[8,3,64]{2,1,0:T(4,128)S(1)}, f32[8,3,64]{2,1,0:T(4,128)S(1)}) all-reduce(f32[8,3,64]{2,1,0:T(4,128)S(1)} %reshape.273, f32[8,3,64]{2,1,0:T(4,128)S(1)} %reshape.274), channel_id=2, replica_groups=mesh['dp'=8,'tensor'=4] {'dp'}, use_global_device_ids=true, to_apply=%region_21.22.clone | all-reduce | flops 3072 | bytes 24576
  608.7 20.5 %all-reduce.15.cloned.1.call-done = bf16[2048,768]{1,0:T(8,128)(2,1)} async-done(((bf16[2048,768]{1,0:T(8,128)(2,1)}), bf16[2048,768]{1,0:T(8,128)(2,1)}) %all-reduce.15.cloned.1.call-update) | async-done | bytes 3145744 | tf_op jit(solution)/shard_map/psum | solution.py:338
  (338 shorter events, 202.0 us)
Async XLA Ops:
  7.2 160.8 %copy-start = (bf16[768,768]{1,0:T(8,128)(2,1)S(1)}, bf16[768,768]{1,0:T(8,128)(2,1)}, u32[]{:S(2)}) copy-start(bf16[768,768]{1,0:T(8,128)(2,1)} %param.25) | copy-start | bytes 3538948
  7.2 9.6 %copy-start.36 = (bf16[768,192]{0,1:T(8,128)(2,1)S(1)}, bf16[768,192]{0,1:T(8,128)(2,1)}, u32[]{:S(2)}) copy-start(bf16[768,192]{0,1:T(8,128)(2,1)} %param.22) | copy-start | bytes 884740
  7.2 151.9 %all-reduce.9.cloned.1.call-start = ((), (), s32[]{:S(2)}) async-start(), calls=%async_computation | async-start | bytes 6291456 | tf_op jit(solution)/shard_map/psum | solution.py:253
  9.0 11.1 %copy-start.44 = (bf16[8,192]{1,0:T(8,128)(2,1)}, bf16[8,192]{1,0:T(8,128)(2,1)S(1)}, u32[]{:S(2)}) copy-start(bf16[8,192]{1,0:T(8,128)(2,1)S(1)} %reshape.272) | copy-start | bytes 9220
  9.8 8.2 %copy-start.46 = (bf16[8,192]{1,0:T(8,128)(2,1)}, bf16[8,192]{1,0:T(8,128)(2,1)S(1)}, u32[]{:S(2)}) copy-start(bf16[8,192]{1,0:T(8,128)(2,1)S(1)} %reshape.269) | copy-start | bytes 9220
  9.8 7.0 %copy-start.4 = (bf16[2048,768]{1,0:T(8,128)(2,1)S(1)}, bf16[2048,768]{1,0:T(8,128)(2,1)}, u32[]{:S(2)}) copy-start(bf16[2048,768]{1,0:T(8,128)(2,1)} %param.19) | copy-start | bytes 9437188
  82.3 80.7 %copy-start.17 = (bf16[3072,192]{0,1:T(8,128)(2,1)}, bf16[3072,192]{0,1:T(8,128)(2,1)S(1)}, u32[]{:S(2)}) copy-start(bf16[3072,192]{0,1:T(8,128)(2,1)S(1)} %get-tuple-element.479) | copy-start | bytes 3538948
  82.3 80.7 %copy-start.18 = (bf16[3072,192]{0,1:T(8,128)(2,1)}, bf16[3072,192]{0,1:T(8,128)(2,1)S(1)}, u32[]{:S(2)}) copy-start(bf16[3072,192]{0,1:T(8,128)(2,1)S(1)} %get-tuple-element.480) | copy-start | bytes 3538948
  87.8 77.6 %copy-start.38 = (f32[768]{0:T(1024)S(1)}, f32[768]{0:T(1024)}, u32[]{:S(2)}) copy-start(f32[768]{0:T(1024)} %param.27) | copy-start | bytes 9220
  87.8 168.8 %all-reduce.11.cloned.1.call-start = ((), (), s32[]{:S(2)}) async-start(), calls=%async_computation.1 | async-start | bytes 6291456 | tf_op jit(solution)/shard_map/psum | solution.py:260
  187.9 68.7 %copy-start.33 = (f32[2048]{0:T(1024)S(1)}, f32[2048]{0:T(1024)}, u32[]{:S(2)}) copy-start(f32[2048]{0:T(1024)} %copy-done.32) | copy-start | bytes 24580
  187.9 180.8 %all-reduce.13.cloned.1.call-start = ((), (), s32[]{:S(2)}) async-start(), calls=%async_computation.2 | async-start | bytes 6291456 | tf_op jit(solution)/shard_map/psum | solution.py:274
  300.0 329.2 %all-reduce.15.cloned.1.call-start = ((), (), s32[]{:S(2)}) async-start(), calls=%async_computation.3 | async-start | bytes 6291456 | tf_op jit(solution)/shard_map/psum | solution.py:338
  368.7 8.4 %copy-start.7 = (bf16[2048,768]{1,0:T(8,128)(2,1)S(1)}, bf16[2048,768]{1,0:T(8,128)(2,1)}, u32[]{:S(2)}) copy-start(bf16[2048,768]{1,0:T(8,128)(2,1)} %param.19) | copy-start | bytes 9437188
  368.7 8.4 %copy-start.10 = (bf16[2048,768]{1,0:T(8,128)(2,1)S(1)}, bf16[2048,768]{1,0:T(8,128)(2,1)}, u32[]{:S(2)}) copy-start(bf16[2048,768]{1,0:T(8,128)(2,1)} %all-reduce.9.cloned.1.call-done) | copy-start | bytes 9437188
  368.7 8.4 %copy-start.26 = (bf16[2048,768]{1,0:T(8,128)(2,1)S(1)}, bf16[2048,768]{1,0:T(8,128)(2,1)}, u32[]{:S(2)}) copy-start(bf16[2048,768]{1,0:T(8,128)(2,1)} %all-reduce.13.cloned.1.call-done) | copy-start | bytes 9437188
  388.6 154.5 %copy-start.47 = (bf16[8,192]{1,0:T(8,128)(2,1)S(1)}, bf16[8,192]{1,0:T(8,128)(2,1)}, u32[]{:S(2)}) copy-start(bf16[8,192]{1,0:T(8,128)(2,1)} %copy-done.46) | copy-start | bytes 9220
  416.7 6.8 %copy-start.23 = (bf16[512,192]{0,1:T(8,128)(2,1)S(1)}, bf16[512,192]{0,1:T(8,128)(2,1)}, u32[]{:S(2)}) copy-start(bf16[512,192]{0,1:T(8,128)(2,1)} %copy-done.22) | copy-start | bytes 589828 | tf_op jit(solution)/shard_map/while
  455.3 6.8 %copy-start.23 = (bf16[512,192]{0,1:T(8,128)(2,1)S(1)}, bf16[512,192]{0,1:T(8,128)(2,1)}, u32[]{:S(2)}) copy-start(bf16[512,192]{0,1:T(8,128)(2,1)} %copy-done.22) | copy-start | bytes 589828 | tf_op jit(solution)/shard_map/while
  493.9 6.8 %copy-start.23 = (bf16[512,192]{0,1:T(8,128)(2,1)S(1)}, bf16[512,192]{0,1:T(8,128)(2,1)}, u32[]{:S(2)}) copy-start(bf16[512,192]{0,1:T(8,128)(2,1)} %copy-done.22) | copy-start | bytes 589828 | tf_op jit(solution)/shard_map/while
  532.4 6.8 %copy-start.23 = (bf16[512,192]{0,1:T(8,128)(2,1)S(1)}, bf16[512,192]{0,1:T(8,128)(2,1)}, u32[]{:S(2)}) copy-start(bf16[512,192]{0,1:T(8,128)(2,1)} %copy-done.22) | copy-start | bytes 589828 | tf_op jit(solution)/shard_map/while
  552.5 8.7 %copy-start.49 = (u32[32]{0:T(128)S(1)}, u32[32]{0:T(128)}, u32[]{:S(2)}) copy-start(u32[32]{0:T(128)} %constant.161) | copy-start | bytes 388
  552.5 10.0 %copy-start.43 = (f32[768]{0:T(1024)S(1)}, f32[768]{0:T(1024)}, u32[]{:S(2)}) copy-start(f32[768]{0:T(1024)} %param.28) | copy-start | bytes 9220
  552.6 79.5 %copy-start.1 = (bf16[768,768]{1,0:T(8,128)(2,1)S(1)}, bf16[768,768]{1,0:T(8,128)(2,1)}, u32[]{:S(2)}) copy-start(bf16[768,768]{1,0:T(8,128)(2,1)} %param.25) | copy-start | bytes 3538948
  (57 other events, 223.3 us)
Sparse Core Ops, SparseCore 0:
  87.9 71.1 all-reduce.8
  188.0 68.5 all-reduce.10
  300.1 68.5 all-reduce.12
  560.6 68.5 all-reduce.14
where the time goes:
time: 649 us; the launch traced here: 639 us
  waiting for transfers between devices  221 us (34%)
  matrix products  173 us (27%)
  other arithmetic  109 us (17%)
  local copies, waits for them, and re-layouts  70.4 us (11%)
  blocking collectives  37 us (6%)
  between operations  15.5 us (2%)
  loops' own time  12.2 us (2%)
    psum x1, waiting for transfers between devices, on_device(): lax.psum(jnp.dot(context, w_out, preferred_element_type=jnp.float32).asty...  71 us
    psum x1, waiting for transfers between devices, on_device(): lax.psum(transpose_dot(grad_pre, w_inner).astype(jnp.bfloat16), 'tensor')  68.6 us
    psum x1, waiting for transfers between devices, on_device(): lax.psum(jnp.dot(active, w_ffn_out, preferred_element_type=jnp.float32).a...  61.1 us
    convert_element_type x4, other arithmetic, attend_backward(): grad_scores = (probability * (grad_prob - row_delta)).astype(jnp.bfloat16)  37.5 us
    unnamed x1, blocking collectives  37 us
    dot_general x8, matrix products, block_scores(): jnp.einsum('qhd,khd->hqk', query_block, key_block, preferred_element_type...  34.9 us
    dot_general x7, matrix products, transpose_dot(): lax.dot_general(left_side, right_side, (((1,), (1,)), ((), ())), preferre...  30 us
    psum x1, waiting for transfers between devices, on_device(): lax.psum(input_term.astype(jnp.bfloat16), 'tensor').astype(jnp.float32)  20.5 us
  transfers between devices with their start and end apart: 4, of which 4 were waited for; matrix products, arithmetic and copies ran while one was open for 3% of the time, Pallas kernels for 0%

commit v1 on v0

--- a/solution.py
+++ b/solution.py
@@ -250,8 +250,12 @@
 
     context_blocks, log_total = lax.map(forward_block, jnp.arange(block_count))
     context = context_blocks.reshape(row_count, col_width).astype(jnp.bfloat16)
-    attn_out = lax.psum(
-        jnp.dot(context, w_out, preferred_element_type=jnp.float32).astype(jnp.bfloat16), "tensor"
+    attn_out = jnp.sum(
+        lax.all_gather(
+            jnp.dot(context, w_out, preferred_element_type=jnp.float32).astype(jnp.bfloat16),
+            "tensor",
+        ),
+        axis=0,
     ).astype(jnp.float32)
     normed, unit_one, inverse_one = normalize(tokens.astype(jnp.float32) + attn_out, gain_attn)
     normed_low = normed.astype(jnp.bfloat16)

time: 649 us -> 673 us (1.037)
  waiting for transfers between devices: 221 us -> 235 us
  other arithmetic: 109 us -> 118 us
    all_gather x0 -> x1, waiting for transfers between devices: none -> 84.7 us  [on_device(): lax.all_gather(jnp.dot(context, w_out, preferred_element_type=jnp.float32...]
    psum x1 -> x0, waiting for transfers between devices: 71 us -> none  [on_device(): lax.psum(jnp.dot(context, w_out, preferred_element_type=jnp.float32).asty...]
    reduce_sum x0 -> x1, other arithmetic: none -> 8.95 us  [on_device(): jnp.sum(lax.all_gather(jnp.dot(context, w_out, preferred_element_type=jnp...]
where the time goes in v1:
time: 673 us; the launch traced here: 663 us
  waiting for transfers between devices  235 us (35%)
  matrix products  173 us (26%)
  other arithmetic  118 us (18%)
  local copies, waits for them, and re-layouts  70.8 us (11%)
  blocking collectives  37 us (5%)
  between operations  15.5 us (2%)
  loops' own time  13.4 us (2%)
    all_gather x1, waiting for transfers between devices, on_device(): lax.all_gather(jnp.dot(context, w_out, preferred_element_type=jnp.float32...  84.7 us
    psum x1, waiting for transfers between devices, on_device(): lax.psum(transpose_dot(grad_pre, w_inner).astype(jnp.bfloat16), 'tensor')  68.7 us
    psum x1, waiting for transfers between devices, on_device(): lax.psum(jnp.dot(active, w_ffn_out, preferred_element_type=jnp.float32).a...  61 us
    convert_element_type x4, other arithmetic, attend_backward(): grad_scores = (probability * (grad_prob - row_delta)).astype(jnp.bfloat16)  37.6 us
    unnamed x1, blocking collectives  37 us
    dot_general x8, matrix products, block_scores(): jnp.einsum('qhd,khd->hqk', query_block, key_block, preferred_element_type...  34.9 us
    dot_general x7, matrix products, transpose_dot(): lax.dot_general(left_side, right_side, (((1,), (1,)), ((), ())), preferre...  30 us
    psum x1, waiting for transfers between devices, on_device(): lax.psum(input_term.astype(jnp.bfloat16), 'tensor').astype(jnp.float32)  20.5 us
  transfers between devices with their start and end apart: 4, of which 4 were waited for; matrix products, arithmetic and copies ran while one was open for 3% of the time, Pallas kernels for 0%

profile of v1, /device:TPU:0, one launch (start us, length us, event | category | flops | bytes accessed | tf_op | source)
XLA Modules:
  0.0 663.4 jit_solution(4611505856906981641)
XLA Ops:
  23.7 59.4 %while.26 = (s32[]{:T(128)}, bf16[4,512,192]{1,2,0:T(8,128)(2,1)}, f32[4,3,512]{2,1,0:T(4,128)}, s32[4]{0:T(128)S(1)}, bf16[3072,192]{0,1:T(8,128)(2,1)S(1)}, /*...) while((s32[]{:T(128)}, bf16[4,512,192]{1,2,0:T(8,128)(2,1)}, ...), condition=%wide.region_5.6_spmd, body=%wide.region_2.5_spmd.sunk | while | flops 638585344 | bytes 36271876 | solution.py:251
  88.8 84.7 %all-gather.3.cloned.1.call-done = bf16[8192,768]{1,0:T(8,128)(2,1)} async-done(((bf16[2048,768]{1,0:T(8,128)(2,1)}), bf16[8192,768]{1,0:T(8,128)(2,1)}) %all-gather.3.cloned.1.call-update) | async-done | bytes 12582928 | tf_op jit(solution)/shard_map/all_gather | solution.py:254
  173.5 8.9 %reduce_sum.114 = bf16[2048,768]{1,0:T(8,128)(2,1)} reduce(bf16[4,2048,768]{2,1,0:T(8,128)(2,1)} %bitcast.175, bf16[]{:T(256)} %constant.86.clone.1), dimensions={0}, to_apply=%region_6.7 | reduce | flops 4718592 | bytes 15728642 | tf_op jit(solution)/shard_map/reduce_sum | solution.py:253
  191.4 19.9 %convolution_convert_fusion.1 = bf16[2048,768]{1,0:T(8,128)(2,1)} fusion(bf16[768,768]{1,0:T(8,128)(2,1)S(1)} %copy-done.46, bf16[2048,768]{1,0:T(8,128)(2,1)} %multiply_convert_fusion.1, bf16[768,768]{1,0:T(8,128)(2,1)S(1)} %copy-done), kind=kOutput, calls=%fused_computation.101 | convolution fusion | flops 4935647232 | bytes 8650752 | tf_op jit(solution)/shard_map/dot_general | solution.py:265
  211.8 7.1 %fusion.131 = f32[2048,768]{1,0:T(8,128)} fusion(bf16[2048,768]{1,0:T(8,128)(2,1)} %multiply_convert_fusion.1, bf16[768,768]{1,0:T(8,128)(2,1)S(1)} %copy-done), kind=kOutput, calls=%fused_computation.218 | convolution fusion | flops 2415919104 | bytes 10616832 | tf_op jit(solution)/shard_map/dot_general | solution.py:273
  218.9 61.0 %all-reduce.8.cloned.1.call-done = bf16[2048,768]{1,0:T(8,128)(2,1)} async-done(((bf16[2048,768]{1,0:T(8,128)(2,1)}), bf16[2048,768]{1,0:T(8,128)(2,1)}) %all-reduce.8.cloned.1.call-update) | async-done | bytes 3145744 | tf_op jit(solution)/shard_map/psum | solution.py:264
  279.9 5.9 fusion.58
  300.7 22.6 %convolution_convert_fusion = bf16[2048,768]{1,0:T(8,128)(2,1)} fusion(bf16[768,768]{1,0:T(8,128)(2,1)S(1)} %copy-done, f32[2048,768]{1,0:T(8,128)} %fusion.131, bf16[768,768]{1,0:T(8,128)(2,1)S(1)} %copy-done.46, f32[2048,768]{1,0:T(8,128)} %subtract_multiply_fusion.1), kind=kOutput, calls=%fused_computation.100 | convolution fusion | flops 4948230144 | bytes 18087936 | tf_op jit(solution)/shard_map/dot_general | solution.py:40
  323.4 68.7 %all-reduce.10.cloned.1.call-done = bf16[2048,768]{1,0:T(8,128)(2,1)} async-done(((bf16[2048,768]{1,0:T(8,128)(2,1)}), bf16[2048,768]{1,0:T(8,128)(2,1)}) %all-reduce.10.cloned.1.call-update) | async-done | bytes 3145744 | tf_op jit(solution)/shard_map/psum | solution.py:278
  392.0 8.3 %fusion.59 = (f32[2048]{0:T(1024)S(1)}, f32[2048]{0:T(1024)S(1)}) fusion(f32[768]{0:T(1024)S(1)} %copy-done.36, f32[2048,768]{1,0:T(8,128)} %subtract_multiply_fusion.1, bf16[2048,768]{1,0:T(8,128)(2,1)} %all-reduce.10.cloned.1.call-done, f32[2048]{0:T(1024)S(1)} %add_rsqrt_fusion.1, f32[2048]{0:T(1024)S(1)} %broadcast_multiply_fusion.5, ...), kind=kLoop, calls=%fused_computation.123 | loop fusion | flops 17297408 | bytes 15764480 | tf_op jit(solution)/shard_map/reduce_sum | solution.py:26
  400.4 5.2 subtract_multiply_fusion
  411.8 155.6 %while.27 = (s32[]{:T(128)}, f32[3072,192]{0,1:T(8,128)}, f32[3072,192]{0,1:T(8,128)S(1)}, bf16[4,512,192]{1,2,0:T(8,128)(2,1)}, s32[4]{0:T(128)}, /*index=5*/bf...) while((s32[]{:T(128)}, f32[3072,192]{0,1:T(8,128)}, ...), condition=%wide.region_19.20_spmd, body=%wide.region_17.19_spmd.sunk | while | flops 1536195072 | bytes 170713200 | solution.py:315
  424.1 6.7 %multiply_reduce_fusion.6 = (f32[3,512]{1,0:T(4,128)S(1)}, f32[3,512,1536]{2,1,0:T(8,128)}) fusion(f32[3,512,1536]{2,1,0:T(8,128)S(1)} %fusion.220, f32[3,512]{1,0:T(4,128)S(1)} %dynamic-slice_bitcast_fusion.2, bf16[512,3,64]{0,2,1:T(8,128)(2,1)S(1)} %bitcast.167, bf16[1536,3,64]{0,2,1:T(8,128)(2,1)S(1)} %bitcast.163, ...), kind=kOutput, calls=%fused_computation.21.clone.1 | convolution fusion | flops 316144128 | bytes 20459520 | tf_op jit(solution)/shard_map/while/body/eval_jaxpr/qhd,khd->hqk/dot_general | solution.py:72
  430.9 9.4 %multiply_convert_fusion.3 = bf16[3,512,1536]{2,1,0:T(8,128)(2,1)} fusion(f32[3,512,1536]{2,1,0:T(8,128)} %get-tuple-element.368, f32[3,512,1536]{2,1,0:T(8,128)} %copy-done.2, f32[3,512]{1,0:T(4,128)S(1)} %get-tuple-element.369), kind=kLoop, calls=%fused_computation.20.clone.1 | loop fusion | flops 7077888 | bytes 23599104 | tf_op jit(solution)/shard_map/while/body/eval_jaxpr/convert_element_type | solution.py:153
  440.3 4.9 fusion.221
  463.0 6.7 %multiply_reduce_fusion.6 = (f32[3,512]{1,0:T(4,128)S(1)}, f32[3,512,1536]{2,1,0:T(8,128)}) fusion(f32[3,512,1536]{2,1,0:T(8,128)S(1)} %fusion.220, f32[3,512]{1,0:T(4,128)S(1)} %dynamic-slice_bitcast_fusion.2, bf16[512,3,64]{0,2,1:T(8,128)(2,1)S(1)} %bitcast.167, bf16[1536,3,64]{0,2,1:T(8,128)(2,1)S(1)} %bitcast.163, ...), kind=kOutput, calls=%fused_computation.21.clone.1 | convolution fusion | flops 316144128 | bytes 20459520 | tf_op jit(solution)/shard_map/while/body/eval_jaxpr/qhd,khd->hqk/dot_general | solution.py:72
  469.7 9.4 %multiply_convert_fusion.3 = bf16[3,512,1536]{2,1,0:T(8,128)(2,1)} fusion(f32[3,512,1536]{2,1,0:T(8,128)} %get-tuple-element.368, f32[3,512,1536]{2,1,0:T(8,128)} %copy-done.2, f32[3,512]{1,0:T(4,128)S(1)} %get-tuple-element.369), kind=kLoop, calls=%fused_computation.20.clone.1 | loop fusion | flops 7077888 | bytes 23599104 | tf_op jit(solution)/shard_map/while/body/eval_jaxpr/convert_element_type | solution.py:153
  501.8 6.7 %multiply_reduce_fusion.6 = (f32[3,512]{1,0:T(4,128)S(1)}, f32[3,512,1536]{2,1,0:T(8,128)}) fusion(f32[3,512,1536]{2,1,0:T(8,128)S(1)} %fusion.220, f32[3,512]{1,0:T(4,128)S(1)} %dynamic-slice_bitcast_fusion.2, bf16[512,3,64]{0,2,1:T(8,128)(2,1)S(1)} %bitcast.167, bf16[1536,3,64]{0,2,1:T(8,128)(2,1)S(1)} %bitcast.163, ...), kind=kOutput, calls=%fused_computation.21.clone.1 | convolution fusion | flops 316144128 | bytes 20459520 | tf_op jit(solution)/shard_map/while/body/eval_jaxpr/qhd,khd->hqk/dot_general | solution.py:72
  508.6 9.4 %multiply_convert_fusion.3 = bf16[3,512,1536]{2,1,0:T(8,128)(2,1)} fusion(f32[3,512,1536]{2,1,0:T(8,128)} %get-tuple-element.368, f32[3,512,1536]{2,1,0:T(8,128)} %copy-done.2, f32[3,512]{1,0:T(4,128)S(1)} %get-tuple-element.369), kind=kLoop, calls=%fused_computation.20.clone.1 | loop fusion | flops 7077888 | bytes 23599104 | tf_op jit(solution)/shard_map/while/body/eval_jaxpr/convert_element_type | solution.py:153
  540.7 6.7 %multiply_reduce_fusion.6 = (f32[3,512]{1,0:T(4,128)S(1)}, f32[3,512,1536]{2,1,0:T(8,128)}) fusion(f32[3,512,1536]{2,1,0:T(8,128)S(1)} %fusion.220, f32[3,512]{1,0:T(4,128)S(1)} %dynamic-slice_bitcast_fusion.2, bf16[512,3,64]{0,2,1:T(8,128)(2,1)S(1)} %bitcast.167, bf16[1536,3,64]{0,2,1:T(8,128)(2,1)S(1)} %bitcast.163, ...), kind=kOutput, calls=%fused_computation.21.clone.1 | convolution fusion | flops 316144128 | bytes 20459520 | tf_op jit(solution)/shard_map/while/body/eval_jaxpr/qhd,khd->hqk/dot_general | solution.py:72
  547.4 9.4 %multiply_convert_fusion.3 = bf16[3,512,1536]{2,1,0:T(8,128)(2,1)} fusion(f32[3,512,1536]{2,1,0:T(8,128)} %get-tuple-element.368, f32[3,512,1536]{2,1,0:T(8,128)} %copy-done.2, f32[3,512]{1,0:T(4,128)S(1)} %get-tuple-element.369), kind=kLoop, calls=%fused_computation.20.clone.1 | loop fusion | flops 7077888 | bytes 23599104 | tf_op jit(solution)/shard_map/while/body/eval_jaxpr/convert_element_type | solution.py:153
  576.9 7.9 %add_convert_fusion = bf16[2048,768]{1,0:T(8,128)(2,1)} fusion(f32[2048,768]{1,0:T(8,128)} %fusion.133, f32[2048,768]{1,0:T(8,128)S(1)} %fusion.125, f32[2048,768]{1,0:T(8,128)S(1)} %fusion.132, f32[2048,768]{1,0:T(8,128)S(1)} %fusion.62, f32[2048,8]{0,1:T(8,128)S(1)} %convolution_multiply_fusion.4, bf16[768,8]{0,1:T(8,128)(2,1)S(1)} %copy-done.38), kind=kOutput, calls=%fused_computation.50 | convolution fusion | flops 158859264 | bytes 28389376 | tf_op jit(solution)/shard_map/dot_general | solution.py:336
  594.7 37.0 %all-reduce.3 = (f32[8,3,64]{2,1,0:T(4,128)S(1)}, f32[8,3,64]{2,1,0:T(4,128)S(1)}) all-reduce(f32[8,3,64]{2,1,0:T(4,128)S(1)} %reshape.273, f32[8,3,64]{2,1,0:T(4,128)S(1)} %reshape.274), channel_id=3, replica_groups=mesh['dp'=8,'tensor'=4] {'dp'}, use_global_device_ids=true, to_apply=%region_21.22.clone | all-reduce | flops 3072 | bytes 24576
  633.1 20.5 %all-reduce.12.cloned.1.call-done = bf16[2048,768]{1,0:T(8,128)(2,1)} async-done(((bf16[2048,768]{1,0:T(8,128)(2,1)}), bf16[2048,768]{1,0:T(8,128)(2,1)}) %all-reduce.12.cloned.1.call-update) | async-done | bytes 3145744 | tf_op jit(solution)/shard_map/psum | solution.py:342
  (335 shorter events, 207.5 us)
Async XLA Ops:
  7.2 184.2 %copy-start = (bf16[768,768]{1,0:T(8,128)(2,1)S(1)}, bf16[768,768]{1,0:T(8,128)(2,1)}, u32[]{:S(2)}) copy-start(bf16[768,768]{1,0:T(8,128)(2,1)} %param.25) | copy-start | bytes 3538948
  7.2 9.6 %copy-start.34 = (bf16[768,192]{0,1:T(8,128)(2,1)S(1)}, bf16[768,192]{0,1:T(8,128)(2,1)}, u32[]{:S(2)}) copy-start(bf16[768,192]{0,1:T(8,128)(2,1)} %param.22) | copy-start | bytes 884740
  7.2 166.3 %all-gather.3.cloned.1.call-start = ((), (), s32[]{:S(2)}) async-start(), calls=%async_computation.3 | async-start | bytes 15728640 | tf_op jit(solution)/shard_map/all_gather | solution.py:254
  9.0 11.1 %copy-start.42 = (bf16[8,192]{1,0:T(8,128)(2,1)}, bf16[8,192]{1,0:T(8,128)(2,1)S(1)}, u32[]{:S(2)}) copy-start(bf16[8,192]{1,0:T(8,128)(2,1)S(1)} %reshape.272) | copy-start | bytes 9220
  9.8 8.2 %copy-start.44 = (bf16[8,192]{1,0:T(8,128)(2,1)}, bf16[8,192]{1,0:T(8,128)(2,1)S(1)}, u32[]{:S(2)}) copy-start(bf16[8,192]{1,0:T(8,128)(2,1)S(1)} %reshape.269) | copy-start | bytes 9220
  9.8 7.0 %copy-start.4 = (bf16[2048,768]{1,0:T(8,128)(2,1)S(1)}, bf16[2048,768]{1,0:T(8,128)(2,1)}, u32[]{:S(2)}) copy-start(bf16[2048,768]{1,0:T(8,128)(2,1)} %param.19) | copy-start | bytes 9437188
  83.1 99.4 %copy-start.17 = (bf16[3072,192]{0,1:T(8,128)(2,1)}, bf16[3072,192]{0,1:T(8,128)(2,1)S(1)}, u32[]{:S(2)}) copy-start(bf16[3072,192]{0,1:T(8,128)(2,1)S(1)} %get-tuple-element.478) | copy-start | bytes 3538948
  83.1 99.4 %copy-start.18 = (bf16[3072,192]{0,1:T(8,128)(2,1)}, bf16[3072,192]{0,1:T(8,128)(2,1)S(1)}, u32[]{:S(2)}) copy-start(bf16[3072,192]{0,1:T(8,128)(2,1)S(1)} %get-tuple-element.479) | copy-start | bytes 3538948
  88.6 191.3 %all-reduce.8.cloned.1.call-start = ((), (), s32[]{:S(2)}) async-start(), calls=%async_computation | async-start | bytes 6291456 | tf_op jit(solution)/shard_map/psum | solution.py:264
  211.3 180.7 %all-reduce.10.cloned.1.call-start = ((), (), s32[]{:S(2)}) async-start(), calls=%async_computation.1 | async-start | bytes 6291456 | tf_op jit(solution)/shard_map/psum | solution.py:278
  323.3 330.3 %all-reduce.12.cloned.1.call-start = ((), (), s32[]{:S(2)}) async-start(), calls=%async_computation.2 | async-start | bytes 6291456 | tf_op jit(solution)/shard_map/psum | solution.py:342
  392.0 8.4 %copy-start.7 = (bf16[2048,768]{1,0:T(8,128)(2,1)S(1)}, bf16[2048,768]{1,0:T(8,128)(2,1)}, u32[]{:S(2)}) copy-start(bf16[2048,768]{1,0:T(8,128)(2,1)} %param.19) | copy-start | bytes 9437188
  392.0 8.4 %copy-start.10 = (bf16[2048,768]{1,0:T(8,128)(2,1)S(1)}, bf16[2048,768]{1,0:T(8,128)(2,1)}, u32[]{:S(2)}) copy-start(bf16[2048,768]{1,0:T(8,128)(2,1)} %reduce_sum.114) | copy-start | bytes 9437188
  392.0 8.4 %copy-start.26 = (bf16[2048,768]{1,0:T(8,128)(2,1)S(1)}, bf16[2048,768]{1,0:T(8,128)(2,1)}, u32[]{:S(2)}) copy-start(bf16[2048,768]{1,0:T(8,128)(2,1)} %all-reduce.10.cloned.1.call-done) | copy-start | bytes 9437188
  411.8 155.6 %copy-start.45 = (bf16[8,192]{1,0:T(8,128)(2,1)S(1)}, bf16[8,192]{1,0:T(8,128)(2,1)}, u32[]{:S(2)}) copy-start(bf16[8,192]{1,0:T(8,128)(2,1)} %copy-done.44) | copy-start | bytes 9220
  424.1 6.7 %copy-start.2 = (f32[3,512,1536]{2,1,0:T(8,128)}, f32[3,512,1536]{2,1,0:T(8,128)S(1)}, u32[]{:S(2)}) copy-start(f32[3,512,1536]{2,1,0:T(8,128)S(1)} %fusion.220) | copy-start | bytes 28311556 | tf_op jit(solution)/shard_map/while
  440.3 6.8 %copy-start.23 = (bf16[512,192]{0,1:T(8,128)(2,1)S(1)}, bf16[512,192]{0,1:T(8,128)(2,1)}, u32[]{:S(2)}) copy-start(bf16[512,192]{0,1:T(8,128)(2,1)} %copy-done.22) | copy-start | bytes 589828 | tf_op jit(solution)/shard_map/while
  463.0 6.7 %copy-start.2 = (f32[3,512,1536]{2,1,0:T(8,128)}, f32[3,512,1536]{2,1,0:T(8,128)S(1)}, u32[]{:S(2)}) copy-start(f32[3,512,1536]{2,1,0:T(8,128)S(1)} %fusion.220) | copy-start | bytes 28311556 | tf_op jit(solution)/shard_map/while
  479.1 6.8 %copy-start.23 = (bf16[512,192]{0,1:T(8,128)(2,1)S(1)}, bf16[512,192]{0,1:T(8,128)(2,1)}, u32[]{:S(2)}) copy-start(bf16[512,192]{0,1:T(8,128)(2,1)} %copy-done.22) | copy-start | bytes 589828 | tf_op jit(solution)/shard_map/while
  518.0 6.8 %copy-start.23 = (bf16[512,192]{0,1:T(8,128)(2,1)S(1)}, bf16[512,192]{0,1:T(8,128)(2,1)}, u32[]{:S(2)}) copy-start(bf16[512,192]{0,1:T(8,128)(2,1)} %copy-done.22) | copy-start | bytes 589828 | tf_op jit(solution)/shard_map/while
  556.8 6.8 %copy-start.23 = (bf16[512,192]{0,1:T(8,128)(2,1)S(1)}, bf16[512,192]{0,1:T(8,128)(2,1)}, u32[]{:S(2)}) copy-start(bf16[512,192]{0,1:T(8,128)(2,1)} %copy-done.22) | copy-start | bytes 589828 | tf_op jit(solution)/shard_map/while
  576.9 8.7 %copy-start.47 = (u32[32]{0:T(128)S(1)}, u32[32]{0:T(128)}, u32[]{:S(2)}) copy-start(u32[32]{0:T(128)} %constant.162) | copy-start | bytes 388
  576.9 10.0 %copy-start.41 = (f32[768]{0:T(1024)S(1)}, f32[768]{0:T(1024)}, u32[]{:S(2)}) copy-start(f32[768]{0:T(1024)} %param.28) | copy-start | bytes 9220
  576.9 79.5 %copy-start.1 = (bf16[768,768]{1,0:T(8,128)(2,1)S(1)}, bf16[768,768]{1,0:T(8,128)(2,1)}, u32[]{:S(2)}) copy-start(bf16[768,768]{1,0:T(8,128)(2,1)} %param.25) | copy-start | bytes 3538948
  (55 other events, 214.6 us)
Sparse Core Ops, SparseCore 0:
  88.7 84.7 all-gather.2
  211.4 68.4 all-reduce.7
  323.4 68.5 all-reduce.9
  585.0 68.5 all-reduce.11
